TPU v7x, 32 devices: a whole 2x2x4 slice. The times are simulated.
32 devices in a mesh: layer: 4 (over y, core), row: 4 (over z), col: 2 (over x).
Axes of the slice: x: 2, y: 2, z: 4, core: 2. Of those that a mesh axis runs over, the one named last changes fastest.
Arguments:
- edge_weight: bfloat16 [2048, 2048], P('row', 'col'), may hold values from 0 to 1, as said below
Outputs:
- clustering: float32 [4, 512], P('row', ('layer', 'col'))
Inputs may be any that keep to these rules, and one draw needn't show every extreme that they name: `edge_weight`: symmetric with a zero diagonal; every vertex v is linked to v - 1 and v + 1 (modulo 2048); an edge's entry lies in [0.2, 1], all other entries are 0.
All inputs are finite; a program needn't handle non-finite values.
Results may differ from a plain program's by a relative error of at most 0.0003.
Values may be sent and summed in bfloat16 or wider, within the bound.
A program may use at most 64 MiB of HBM per device.

v0:
```python
import jax
import jax.numpy as jnp
from jax import lax
from jax.sharding import PartitionSpec as P

STRIPE = 128


def local(edge_weight):
    layers = lax.axis_size("layer")
    layer_index = lax.axis_index("layer")
    row_count, col_count = edge_weight.shape
    row_global = lax.axis_index("row") * row_count + jnp.arange(row_count, dtype=jnp.int32)
    col_global = lax.axis_index("col") * col_count + jnp.arange(col_count, dtype=jnp.int32)
    lower = jnp.where(
        row_global[:, None] > col_global[None, :], edge_weight, jnp.zeros_like(edge_weight)
    )
    column_groups = lower.reshape(row_count, col_count // (STRIPE * layers), layers, STRIPE)
    left_local = lax.dynamic_index_in_dim(column_groups, layer_index, 2, keepdims=False).reshape(
        row_count, col_count // layers
    )
    row_groups = lower.reshape(row_count // (STRIPE * layers), layers, STRIPE, col_count)
    right_local = lax.dynamic_index_in_dim(row_groups, layer_index, 1, keepdims=False).reshape(
        row_count // layers, col_count
    )
    left_whole = lax.all_gather(left_local, "col", axis=1, tiled=True)
    right_whole = lax.all_gather(right_local, "row", axis=0, tiled=True)
    paths = jnp.dot(left_whole, right_whole, preferred_element_type=jnp.float32)
    triangles = jnp.sum(paths * lower, axis=1)
    degree = jnp.sum(jnp.where(left_local > 0, 1.0, 0.0).astype(jnp.float32), axis=1)
    layer_share = (
        lax.psum_scatter(triangles, "layer", scatter_dimension=0, tiled=True),
        lax.psum_scatter(degree, "layer", scatter_dimension=0, tiled=True),
    )
    tri_total, degree_total = (
        lax.psum_scatter(layer_share[0], "col", scatter_dimension=0, tiled=True),
        lax.psum_scatter(layer_share[1], "col", scatter_dimension=0, tiled=True),
    )
    clustering = 2.0 * tri_total / jnp.maximum(degree_total * (degree_total - 1.0), 2.0)
    return clustering.reshape(1, -1)


def solution(mesh):
    placed = (P("row", "col"),)
    return jax.shard_map(
        local, mesh=mesh, in_specs=placed, out_specs=P("row", ("layer", "col")), check_vma=False
    )
```

profile of v0, /device:TPU:0, one launch (start us, length us, event | category | flops | bytes accessed | tf_op | source)
XLA Modules:
  0.0 60.3 jit_solution(14782072480402922622)
XLA Ops:
  6.5 0.0 all-gather.3.cloned.1.call-start
  6.5 1.5 %compare_select_fusion = bf16[512,1024]{1,0:T(8,128)(2,1)S(1)} fusion(bf16[512,1024]{1,0:T(8,128)(2,1)} %param.1, s32[1024]{0:T(1024)S(1)} %iota_add_fusion, s32[512]{0:T(512)S(1)} %iota_add_fusion.1), kind=kLoop, calls=%fused_computation.1 | loop fusion | flops 1048576 | bytes 2103296 | tf_op jit(solution)/shard_map/jit(_where)/select_n | solution.py:15
  8.1 0.7 %constant_dynamic-slice_fusion = bf16[1,1,128,1024]{3,2,1,0:T(8,128)(2,1)} fusion(bf16[1,4,128,1024]{3,2,1,0:T(8,128)(2,1)S(1)} %bitcast.10, s32[]{:T(128)S(6)} %select_n.16), kind=kLoop, calls=%fused_computation.10 | loop fusion | bytes 524292 | tf_op jit(solution)/shard_map/jit(dynamic_index_in_dim)/dynamic_slice | solution.py:23
  8.8 0.0 all-gather.3.cloned.1.call-update
  8.8 0.8 %reshape.25 = bf16[512,2,4,128]{3,2,1,0:T(4,128)(2,1)S(1)} reshape(bf16[512,1024]{1,0:T(8,128)(2,1)S(1)} %compare_select_fusion) | data formatting | bytes 2097152 | tf_op jit(solution)/shard_map/reshape | solution.py:18
  9.6 0.0 copy-start.1
  9.6 0.0 copy-start
  9.7 0.5 constant_dynamic-slice_fusion.1
  10.2 0.7 %copy.4 = bf16[512,2,1,128]{0,3,1,2:T(8,128)(2,1)S(1)} copy(bf16[512,2,1,128]{3,2,1,0:T(2,128)(2,1)S(1)} %constant_dynamic-slice_fusion.1) | data formatting | bytes 524288
  10.9 0.0 copy-done.1
  10.9 0.6 dynamic-slice
  11.5 0.0 copy-done
  11.5 0.6 %dynamic-slice.2 = u32[1]{0:T(128)} dynamic-slice(u32[32]{0:T(128)S(1)} %copy-done, u32[]{:T(128)S(6)} %add.41), dynamic_slice_sizes={1} | dynamic-slice | bytes 12
  13.4 9.9 %all_gather.6 = bf16[512,512]{0,1:T(8,128)(2,1)S(1)} all-gather(bf16[512,256]{0,1:T(8,128)(2,1)S(1)} %bitcast.11), channel_id=1, replica_groups=mesh['layer'=4,'row'=4,'col'=2] {'col'}, dimensions={1}, use_global_device_ids=true | all-gather | bytes 786432 | tf_op jit(solution)/shard_map/all_gather | solution.py:26
  23.3 0.1 select_reduce_fusion
  23.4 16.3 %all-gather.3.cloned.1.call-done = bf16[1,1,512,1024]{3,2,1,0:T(8,128)(2,1)} async-done(((bf16[1,1,128,1024]{3,2,1,0:T(8,128)(2,1)}), bf16[1,1,512,1024]{3,2,1,0:T(8,128)(2,1)}) %all-gather.3.cloned.1.call-update) | async-done | bytes 1048592 | tf_op jit(solution)/shard_map/all_gather | solution.py:27
  39.7 2.0 %multiply_reduce_fusion = f32[512]{0:T(512)S(1)} fusion(bf16[512,1024]{1,0:T(8,128)(2,1)S(1)} %compare_select_fusion, bf16[512,512]{0,1:T(8,128)(2,1)S(1)} %all_gather.6, bf16[1,1,512,1024]{3,2,1,0:T(8,128)(2,1)} %all-gather.3.cloned.1.call-done), kind=kOutput, calls=%fused_computation | convolution fusion | flops 538443264 | bytes 2623488 | tf_op jit(solution)/shard_map/dot_general | solution.py:28
  41.7 6.1 %all-reduce.4 = (f32[512]{0:T(512)S(1)}, f32[512]{0:T(512)S(1)}) all-reduce(f32[512]{0:T(512)S(1)} %select_reduce_fusion, f32[512]{0:T(512)S(1)} %multiply_reduce_fusion), channel_id=5, replica_groups=mesh['layer'=4,'row'=4,'col'=2] {'layer'}, use_global_device_ids=true, to_apply=%region_4.5.clone | all-reduce | flops 1024 | bytes 8192
  47.8 0.1 dynamic-slice.5
  47.9 0.1 dynamic-slice.1
  48.0 4.9 %all-reduce.5 = (f32[128]{0:T(128)S(1)}, f32[128]{0:T(128)S(1)}) all-reduce(f32[128]{0:T(128)S(1)} %dynamic-slice.5, f32[128]{0:T(128)S(1)} %dynamic-slice.1), channel_id=6, replica_groups=mesh['layer'=4,'row'=4,'col'=2] {'col'}, use_global_device_ids=true, to_apply=%region_5.6.clone | all-reduce | flops 256 | bytes 2048
  52.9 0.6 fusion.3
  (2 shorter events, 0.0 us)
Async XLA Ops:
  6.5 33.2 %all-gather.3.cloned.1.call-start = ((), (), s32[]{:S(2)}) async-start(), calls=%async_computation | async-start | bytes 1310720 | tf_op jit(solution)/shard_map/all_gather | solution.py:27
  9.6 1.3 %copy-start.1 = (u32[32]{0:T(128)S(1)}, u32[32]{0:T(128)}, u32[]{:S(2)}) copy-start(u32[32]{0:T(128)} %constant.39) | copy-start | bytes 388
  9.6 1.9 %copy-start = (u32[32]{0:T(128)S(1)}, u32[32]{0:T(128)}, u32[]{:S(2)}) copy-start(u32[32]{0:T(128)} %constant.43) | copy-start | bytes 388
Sparse Core Ops, SparseCore 0:
  9.0 30.6 all-gather.2
where the time goes:
time: 60.6 us; the launch traced here: 60.3 us
  blocking collectives  20.9 us (34%)
  waiting for transfers between devices  16.3 us (27%)
  between operations  14.7 us (24%)
  local copies, waits for them, and re-layouts  4.1 us (7%)
  other arithmetic  2.22 us (4%)
  matrix products  2.04 us (3%)
    all_gather x1, waiting for transfers between devices, local(): right_whole = lax.all_gather(right_local, 'row', axis=0, tiled=True)  16.3 us
    unnamed x2, blocking collectives  11 us
    all_gather x1, blocking collectives, local(): left_whole = lax.all_gather(left_local, 'col', axis=1, tiled=True)  9.94 us
    unnamed x9, local copies, waits for them, and re-layouts  2.05 us
    dot_general x1, matrix products, local(): paths = jnp.dot(left_whole, right_whole, preferred_element_type=jnp.float32)  2.04 us
    select_n x1, other arithmetic, local(): jnp.where(row_global[:, None] > col_global[None, :], edge_weight, jnp.zer...  1.53 us
  transfers between devices with their start and end apart: 1, of which 1 were waited for; matrix products, arithmetic and copies ran while one was open for 5% of the time, Pallas kernels for 0%

commit v1 on v0

--- a/solution.py
+++ b/solution.py
@@ -24,7 +24,12 @@
         row_count // layers, col_count
     )
     left_whole = lax.all_gather(left_local, "col", axis=1, tiled=True)
-    right_whole = lax.all_gather(right_local, "row", axis=0, tiled=True)
+    ring = [right_local]
+    for hop in range(3):
+        ring.append(lax.ppermute(ring[-1], "row", [(dev, (dev + 1) % 4) for dev in range(4)]))
+    right_whole = jnp.roll(
+        jnp.concatenate(ring[::-1], axis=0), (lax.axis_index("row") + 1) * ring[0].shape[0], axis=0
+    )
     paths = jnp.dot(left_whole, right_whole, preferred_element_type=jnp.float32)
     triangles = jnp.sum(paths * lower, axis=1)
     degree = jnp.sum(jnp.where(left_local > 0, 1.0, 0.0).astype(jnp.float32), axis=1)

time: 60.6 us -> 43.3 us (0.71)
  between operations: 14.7 us -> 1.5 us
  starting transfers between devices: 0.01 us -> 3.12 us
  blocking collectives: 20.9 us -> 17.8 us
  waiting for transfers between devices: 16.3 us -> 14 us
  matrix products: 2.04 us -> 0.82 us
    all_gather x1 -> x0, waiting for transfers between devices: 16.3 us -> none  [local(): right_whole = lax.all_gather(right_local, 'row', axis=0, tiled=True)]
    ppermute x0 -> x3, waiting for transfers between devices: none -> 14 us  [local(): lax.ppermute(ring[-1], 'row', [(dev, (dev + 1) % 4) for dev in range(4)])]
    ppermute x0 -> x3, starting transfers between devices: none -> 3.12 us  [local(): lax.ppermute(ring[-1], 'row', [(dev, (dev + 1) % 4) for dev in range(4)])]
    all_gather x1, blocking collectives: 9.94 us -> 7.27 us  [local(): left_whole = lax.all_gather(left_local, 'col', axis=1, tiled=True)]
    dot_general x1, matrix products: 2.04 us -> 0.82 us  [local(): paths = jnp.dot(left_whole, right_whole, preferred_element_type=jnp.float32)]
    dynamic_slice x1 -> x0, local copies, waits for them, and re-layouts: 0.74 us -> none  [local(): lax.dynamic_index_in_dim(row_groups, layer_index, 1, keepdims=False)]
    unnamed x9 -> x16, local copies, waits for them, and re-layouts: 2.05 us -> 2.23 us
  transfers between devices with their start and end apart: 1 -> 3, of which waited for: 1 -> 3; matrix products, arithmetic and copies ran while one was open for 5% -> 8% of each run, Pallas kernels for 0% -> 0%
where the time goes in v1:
time: 43.3 us; the launch traced here: 43.1 us
  blocking collectives  17.8 us (41%)
  waiting for transfers between devices  14 us (32%)
  local copies, waits for them, and re-layouts  3.58 us (8%)
  starting transfers between devices  3.12 us (7%)
  other arithmetic  2.22 us (5%)
  between operations  1.5 us (3%)
  matrix products  0.82 us (2%)
    ppermute x3, waiting for transfers between devices, local(): lax.ppermute(ring[-1], 'row', [(dev, (dev + 1) % 4) for dev in range(4)])  14 us
    unnamed x2, blocking collectives  10.6 us
    all_gather x1, blocking collectives, local(): left_whole = lax.all_gather(left_local, 'col', axis=1, tiled=True)  7.27 us
    ppermute x3, starting transfers between devices, local(): lax.ppermute(ring[-1], 'row', [(dev, (dev + 1) % 4) for dev in range(4)])  3.12 us
    unnamed x16, local copies, waits for them, and re-layouts  2.23 us
    select_n x1, other arithmetic, local(): jnp.where(row_global[:, None] > col_global[None, :], edge_weight, jnp.zer...  1.53 us
  transfers between devices with their start and end apart: 3, of which 3 were waited for; matrix products, arithmetic and copies ran while one was open for 8% of the time, Pallas kernels for 0%

profile of v1, /device:TPU:0, one launch (start us, length us, event | category | flops | bytes accessed | tf_op | source)
XLA Modules:
  0.0 43.1 jit_solution(4070823181122152081)
XLA Ops:
  0.0 1.5 %compare_select_fusion = bf16[512,1024]{1,0:T(8,128)(2,1)S(1)} fusion(bf16[512,1024]{1,0:T(8,128)(2,1)} %param.1, s32[1024]{0:T(1024)S(1)} %iota_add_fusion, s32[512]{0:T(512)S(1)} %iota_add_fusion.1), kind=kLoop, calls=%fused_computation.1 | loop fusion | flops 1048576 | bytes 2103296 | tf_op jit(solution)/shard_map/jit(_where)/select_n | solution.py:15
  1.6 0.0 copy-start.1
  1.6 0.0 copy-start
  1.6 3.1 %collective-permute-start = (bf16[128,1024]{1,0:T(8,128)(2,1)S(1)}, bf16[128,1024]{1,0:T(8,128)(2,1)S(1)}, u32[]{:S(2)}, u32[]{:S(2)}) collective-permute-start(bf16[128,1024]{1,0:T(8,128)(2,1)S(1)} %dynamic-slice_bitcast_fusion), channel_id=1, source_target_pairs={{0,2},{2,4},{4,6},{6,0},{1,3},{3,5},{5,7},{7,1},{8,10},{10,12},{12... | collective-permute-start | bytes 786440 | tf_op jit(solution)/shard_map/ppermute | solution.py:29
  4.7 8.3 %collective-permute-done = bf16[128,1024]{1,0:T(8,128)(2,1)S(1)} collective-permute-done((bf16[128,1024]{1,0:T(8,128)(2,1)S(1)}, bf16[128,1024]{1,0:T(8,128)(2,1)S(1)}, u32[]{:S(2)}, u32[]{:S(2)}) %collective-permute-start) | collective-permute-done | bytes 262176 | tf_op jit(solution)/shard_map/ppermute | solution.py:29
  13.0 0.0 collective-permute-start.1
  13.0 0.7 %reshape.25 = bf16[512,2,4,128]{3,2,1,0:T(4,128)(2,1)S(1)} reshape(bf16[512,1024]{1,0:T(8,128)(2,1)S(1)} %compare_select_fusion) | data formatting | bytes 2097152 | tf_op jit(solution)/shard_map/reshape | solution.py:18
  13.8 0.5 %constant_dynamic-slice_fusion = bf16[512,2,1,128]{3,2,1,0:T(2,128)(2,1)S(1)} fusion(bf16[512,2,4,128]{3,2,1,0:T(4,128)(2,1)S(1)} %reshape.25, s32[]{:T(128)S(6)} %select_n.29), kind=kLoop, calls=%fused_computation.17 | loop fusion | bytes 524292 | tf_op jit(solution)/shard_map/jit(dynamic_index_in_dim)/dynamic_slice | solution.py:19
  14.4 0.7 %copy.4 = bf16[512,2,1,128]{0,3,1,2:T(8,128)(2,1)S(1)} copy(bf16[512,2,1,128]{3,2,1,0:T(2,128)(2,1)S(1)} %constant_dynamic-slice_fusion) | data formatting | bytes 524288
  15.1 0.0 copy-done.1
  15.1 0.6 %dynamic-slice = u32[1]{0:T(128)} dynamic-slice(u32[32]{0:T(128)S(1)} %copy-done.1, u32[]{:T(128)S(6)} %add.57), dynamic_slice_sizes={1} | dynamic-slice | bytes 12
  15.7 0.0 copy-done
  15.7 0.7 %dynamic-slice.2 = u32[1]{0:T(128)} dynamic-slice(u32[32]{0:T(128)S(1)} %copy-done, u32[]{:T(128)S(6)} %add.57), dynamic_slice_sizes={1} | dynamic-slice | bytes 12
  17.7 4.6 %collective-permute-done.1 = bf16[128,1024]{1,0:T(8,128)(2,1)S(1)} collective-permute-done((bf16[128,1024]{1,0:T(8,128)(2,1)S(1)}, bf16[128,1024]{1,0:T(8,128)(2,1)S(1)}, u32[]{:S(2)}, u32[]{:S(2)}) %collective-permute-start.1) | collective-permute-done | bytes 262176 | tf_op jit(solution)/shard_map/ppermute | solution.py:29
  22.3 0.0 collective-permute-start.2
  22.3 7.3 %all_gather.3 = bf16[512,512]{0,1:T(8,128)(2,1)S(1)} all-gather(bf16[512,256]{0,1:T(8,128)(2,1)S(1)} %bitcast.16), channel_id=1, replica_groups=mesh['layer'=4,'row'=4,'col'=2] {'col'}, dimensions={1}, use_global_device_ids=true | all-gather | bytes 786432 | tf_op jit(solution)/shard_map/all_gather | solution.py:26
  29.6 0.1 select_reduce_fusion
  29.7 1.0 %collective-permute-done.2 = bf16[128,1024]{1,0:T(8,128)(2,1)S(1)} collective-permute-done((bf16[128,1024]{1,0:T(8,128)(2,1)S(1)}, bf16[128,1024]{1,0:T(8,128)(2,1)S(1)}, u32[]{:S(2)}, u32[]{:S(2)}) %collective-permute-start.2) | collective-permute-done | bytes 262176 | tf_op jit(solution)/shard_map/ppermute | solution.py:29
  31.0 0.8 %multiply_reduce_fusion = f32[512]{0:T(512)S(1)} fusion(bf16[512,1024]{1,0:T(8,128)(2,1)S(1)} %compare_select_fusion, bf16[512,512]{0,1:T(8,128)(2,1)S(1)} %all_gather.3, bf16[1024,1024]{1,0:T(8,128)(2,1)S(1)} %constant_dynamic-update-slice_fusion, s32[]{:T(128)S(6)} %select_n.31), kind=kOutput, calls=%fused_computation | convolution fusion | flops 538443264 | bytes 2623492 | tf_op jit(solution)/shard_map/dot_general | solution.py:33
  31.8 5.7 %all-reduce.4 = (f32[512]{0:T(512)S(1)}, f32[512]{0:T(512)S(1)}) all-reduce(f32[512]{0:T(512)S(1)} %select_reduce_fusion, f32[512]{0:T(512)S(1)} %multiply_reduce_fusion), channel_id=4, replica_groups=mesh['layer'=4,'row'=4,'col'=2] {'layer'}, use_global_device_ids=true, to_apply=%region_4.5.clone | all-reduce | flops 1024 | bytes 8192
  37.4 0.1 dynamic-slice.1
  37.5 0.1 dynamic-slice.5
  37.6 4.9 %all-reduce.5 = (f32[128]{0:T(128)S(1)}, f32[128]{0:T(128)S(1)}) all-reduce(f32[128]{0:T(128)S(1)} %dynamic-slice.5, f32[128]{0:T(128)S(1)} %dynamic-slice.1), channel_id=5, replica_groups=mesh['layer'=4,'row'=4,'col'=2] {'col'}, use_global_device_ids=true, to_apply=%region_5.6.clone | all-reduce | flops 256 | bytes 2048
  42.5 0.6 %fusion.4 = f32[1,64]{1,0:T(1,128)} fusion(f32[128]{0:T(128)S(1)} %get-tuple-element.7, u32[]{:T(128)S(6)} %multiply.3, f32[128]{0:T(128)S(1)} %get-tuple-element.8), kind=kLoop, calls=%fused_computation.21 | loop fusion | flops 320 | bytes 772 | tf_op jit(solution)/shard_map/reshape | solution.py:45
  (11 shorter events, 0.2 us)
Async XLA Ops:
  1.6 13.5 %copy-start.1 = (u32[32]{0:T(128)S(1)}, u32[32]{0:T(128)}, u32[]{:S(2)}) copy-start(u32[32]{0:T(128)} %constant.63) | copy-start | bytes 388
  1.6 14.1 %copy-start = (u32[32]{0:T(128)S(1)}, u32[32]{0:T(128)}, u32[]{:S(2)}) copy-start(u32[32]{0:T(128)} %constant.67) | copy-start | bytes 388
  1.6 11.4 %collective-permute-start = (bf16[128,1024]{1,0:T(8,128)(2,1)S(1)}, bf16[128,1024]{1,0:T(8,128)(2,1)S(1)}, u32[]{:S(2)}, u32[]{:S(2)}) collective-permute-start(bf16[128,1024]{1,0:T(8,128)(2,1)S(1)} %dynamic-slice_bitcast_fusion), channel_id=1, source_target_pairs={{0,2},{2,4},{4,6},{6,0},{1,3},{3,5},{5,7},{7,1},{8,10},{10,12},{12... | collective-permute-start | bytes 786440 | tf_op jit(solution)/shard_map/ppermute | solution.py:29
  13.0 9.3 %collective-permute-start.1 = (bf16[128,1024]{1,0:T(8,128)(2,1)S(1)}, bf16[128,1024]{1,0:T(8,128)(2,1)S(1)}, u32[]{:S(2)}, u32[]{:S(2)}) collective-permute-start(bf16[128,1024]{1,0:T(8,128)(2,1)S(1)} %collective-permute-done), channel_id=1, source_target_pairs={{0,2},{2,4},{4,6},{6,0},{1,3},{3,5},{5,7},{7,1},{8,10},{10,12},{12... | collective-permute-start | bytes 786440 | tf_op jit(solution)/shard_map/ppermute | solution.py:29
  22.3 8.4 %collective-permute-start.2 = (bf16[128,1024]{1,0:T(8,128)(2,1)S(1)}, bf16[128,1024]{1,0:T(8,128)(2,1)S(1)}, u32[]{:S(2)}, u32[]{:S(2)}) collective-permute-start(bf16[128,1024]{1,0:T(8,128)(2,1)S(1)} %collective-permute-done.1), channel_id=1, source_target_pairs={{0,2},{2,4},{4,6},{6,0},{1,3},{3,5},{5,7},{7,1},{8,10},{10,12},{12... | collective-permute-start | bytes 786440 | tf_op jit(solution)/shard_map/ppermute | solution.py:29
